TPU v7x, 128 devices: a whole 4x4x4 slice. The times are simulated.
128 devices in a mesh: segment: 2 (over x_lo), seq: 16 (over z, y), mp: 4 (over x_hi, core).
Axes of the slice: x: 4 (x_hi: 2, x_lo: 2; x = x_hi * 2 + x_lo), y: 4, z: 4, core: 2. Of those that a mesh axis runs over, the one named last changes fastest.
Arguments:
- memory: bfloat16 [2, 4096, 4096], P(None, 'seq', 'mp')
- decoder_rows: bfloat16 [2, 1024, 4096], P(None, 'seq', 'mp')
- gains: bfloat16 [2, 4096], P('segment'), may hold values from 0.5 to 1.5
- weights: bfloat16 [2, 2, 4096, 4096], P('segment', None, None, 'mp')
- lengths: int32 [2], replicated, may hold values from 512 to 4096, as said below
Outputs:
- decoder_out: bfloat16 [2, 1024, 4096], P(None, 'seq', ('segment', 'mp'))
Inputs may be any that keep to these rules, and one draw needn't show every extreme that they name: memory positions of document b at or beyond lengths[b] are padding; some document has all 4096 positions.
All inputs are finite; a program needn't handle non-finite values.
Results may differ from a plain program's by a relative error of at most 0.015.
The roundings to bfloat16 on the way count: a program that leaves them out, or rounds other values in their place, can miss the bound.
Values may be sent and summed in bfloat16 or wider, within the bound.
A program may use at most 192 MiB of HBM per device.

v0:
```python
import jax
import jax.numpy as jnp
from jax import lax
from jax.sharding import PartitionSpec as P

DKV = 64
norm_eps = 1e-06
masked_score = -1e30


def passed_along(shard, axis, by):
    count = lax.axis_size(axis)
    pairs = [(i, i + by) for i in range(count) if 0 <= i + by < count]
    return lax.ppermute(shard, axis, pairs)


def rms_rows(rows, gain):
    wide = rows.astype(jnp.float32)
    inverse = lax.rsqrt(jnp.mean(wide * wide, axis=1, keepdims=True) + norm_eps)
    return (wide * inverse * gain.astype(jnp.float32)[None, :]).astype(jnp.bfloat16)


def fold_block(running, queries, key_block, value_block, first_pos, lengths):
    maxima, totals, summed = running
    doc_count, span = (key_block.shape[0], key_block.shape[1])
    heads_here = queries.shape[2]
    key_heads = key_block.reshape(doc_count, span, heads_here, DKV)
    value_heads = value_block.reshape(doc_count, span, heads_here, DKV)
    scores = jnp.einsum("bqhd,bkhd->bhqk", queries, key_heads, preferred_element_type=jnp.float32)
    positions = first_pos + lax.iota(jnp.int32, span)
    valid_keys = (positions[None, :] < lengths[:, None])[:, None, None, :]
    masked = jnp.where(valid_keys, scores, masked_score)
    new_max = jnp.maximum(maxima, jnp.max(masked, axis=-1))
    exp_scores = jnp.where(valid_keys, jnp.exp(masked - new_max[..., None]), 0.0)
    rescale = jnp.exp(maxima - new_max)
    totals = totals * rescale + jnp.sum(exp_scores, axis=-1)
    summed = summed * rescale[..., None] + jnp.einsum(
        "bhqk,bkhd->bhqd",
        exp_scores.astype(jnp.bfloat16),
        value_heads,
        preferred_element_type=jnp.float32,
    )
    return (new_max, totals, summed)


def on_device(memory, decoder_rows, gains, weights, lengths):
    segment_index = lax.axis_index("segment")
    decoding = segment_index == 1
    doc_count, mem_dev, part_width = memory.shape
    pos_dev = decoder_rows.shape[1]
    mem_count = doc_count * mem_dev
    row_count = doc_count * pos_dev
    mem_full, dec_full = (
        lax.all_gather(memory.reshape(mem_count, part_width), "mp", axis=1, tiled=True),
        lax.all_gather(decoder_rows.reshape(row_count, part_width), "mp", axis=1, tiled=True),
    )
    first_weight = weights[0, 0]
    second_weight = weights[0, 1]
    section_gain = gains[0]
    head_width = first_weight.shape[1]
    heads_here = head_width // DKV

    def encode(source):
        normed = rms_rows(source, section_gain)
        key_out = jnp.dot(normed, first_weight, preferred_element_type=jnp.float32).astype(
            jnp.bfloat16
        )
        value_out = jnp.dot(normed, second_weight, preferred_element_type=jnp.float32).astype(
            jnp.bfloat16
        )
        return (key_out, value_out)

    def skip_encode(source):
        empty = jnp.zeros((mem_count, head_width), jnp.bfloat16)
        return (empty, empty)

    key_local, value_local = lax.cond(decoding, skip_encode, encode, mem_full)
    query_rows = lax.cond(
        decoding,
        lambda source: jnp.dot(
            rms_rows(source, section_gain), first_weight, preferred_element_type=jnp.float32
        ).astype(jnp.bfloat16),
        lambda source: jnp.zeros((row_count, head_width), jnp.bfloat16),
        dec_full,
    )
    key_rows, value_rows = passed_along((key_local, value_local), "segment", 1)
    key_flat = key_rows.reshape(doc_count, mem_dev, head_width)
    value_flat = value_rows.reshape(doc_count, mem_dev, head_width)
    queries = query_rows.reshape(doc_count, pos_dev, heads_here, DKV)
    start_state = (
        jnp.full((doc_count, heads_here, pos_dev), masked_score, jnp.float32),
        jnp.zeros((doc_count, heads_here, pos_dev), jnp.float32),
        jnp.zeros((doc_count, heads_here, pos_dev, DKV), jnp.float32),
    )
    first_pos = jnp.int32(0)
    key_part = lax.all_gather(key_flat, "seq", axis=1, tiled=True)
    value_part = lax.all_gather(value_flat, "seq", axis=1, tiled=True)
    span = key_part.shape[1]
    width = 256

    def attend(state):
        for offset in range(0, span, width):
            state = fold_block(
                state,
                queries,
                key_part[:, offset : offset + width],
                value_part[:, offset : offset + width],
                first_pos + offset,
                lengths,
            )
        return state

    final_state = lax.cond(decoding, attend, lambda state: state, start_state)

    def finish(state):
        context = state[2] / state[1][..., None]
        return (
            jnp.transpose(context, (0, 2, 1, 3)).reshape(row_count, head_width).astype(jnp.bfloat16)
        )

    context_rows = lax.cond(
        decoding,
        finish,
        lambda state: jnp.zeros((row_count, head_width), jnp.bfloat16),
        final_state,
    )
    update_terms = lax.cond(
        decoding,
        lambda source: lax.dot_general(
            source, second_weight, (((1,), (1,)), ((), ())), preferred_element_type=jnp.float32
        ),
        lambda source: jnp.zeros((row_count, second_weight.shape[0]), jnp.float32),
        context_rows,
    )
    update = lax.psum_scatter(
        update_terms.astype(jnp.bfloat16), ("segment", "mp"), scatter_dimension=1, tiled=True
    ).astype(jnp.float32)
    out_width = update.shape[1]
    group_index = segment_index * lax.axis_size("mp") + lax.axis_index("mp")
    residual = lax.dynamic_slice_in_dim(dec_full, group_index * out_width, out_width, 1)
    decoder_out = (residual.astype(jnp.float32) + update).astype(jnp.bfloat16)
    return decoder_out.reshape(doc_count, pos_dev, out_width)


def solution(mesh):
    in_specs = (
        P(None, "seq", "mp"),
        P(None, "seq", "mp"),
        P("segment", None),
        P("segment", None, None, "mp"),
        P(),
    )
    out_specs = P(None, "seq", ("segment", "mp"))
    return jax.shard_map(
        on_device, mesh=mesh, in_specs=in_specs, out_specs=out_specs, check_vma=False
    )
```

profile of v0, /device:TPU:1, one launch (start us, length us, event | category | flops | bytes accessed | tf_op | source)
XLA Modules:
  0.0 470.3 jit_solution(12025478866281575327)
XLA Ops:
  6.5 0.7 all-gather.7.cloned.1.call-update
  7.3 0.0 all-gather.5.cloned.1.call-start
  7.3 0.7 all-gather.5.cloned.1.call-update
  8.0 0.0 all-gather.9.cloned.1.call-start
  8.1 11.7 %slice_bitcast_fusion = (bf16[4096,1024]{1,0:T(8,128)(2,1)}, bf16[4096,1024]{1,0:T(8,128)(2,1)}) fusion(bf16[1,2,4096,1024]{3,2,1,0:T(8,128)(2,1)} %param.18), kind=kLoop, calls=%fused_computation.292 | loop fusion | bytes 33554432 | tf_op jit(solution)/shard_map/squeeze | solution.py:58
  19.8 0.1 reduce
  19.8 31.4 %all-gather.7.cloned.1.call-done = bf16[512,4096]{1,0:T(8,128)(2,1)} async-done(((bf16[512,1024]{1,0:T(8,128)(2,1)}), bf16[512,4096]{1,0:T(8,128)(2,1)}) %all-gather.7.cloned.1.call-update) | async-done | bytes 4194320 | tf_op jit(solution)/shard_map/all_gather | solution.py:54
  51.2 17.2 %conditional.5 = (bf16[512,1024]{1,0:T(8,128)(2,1)S(1)}, bf16[512,1024]{1,0:T(8,128)(2,1)S(1)}) conditional(s32[]{:T(128)} %convert_element_type.104, (bf16[512,4096]{1,0:T(8,128)(2,1)}, bf16[4096]{0:T(1024)(128)(2,1)S(1)}, bf16[4096,1024]{1,0:T(8,128)(2,1)}, bf16[4096,1024]{1,0:T(8,128)(2,1)}) %tuple.43, () %tuple.44), branch_computations={%region_0.0_spmd, %region_2.0_spmd} | conditional | flops 8614055936 | bytes 73468000 | solution.py:77
  51.2 3.2 fusion
  54.5 9.3 %convolution_convert_fusion = bf16[512,1024]{1,0:T(8,128)(2,1)S(1)} fusion(bf16[4096,1024]{1,0:T(8,128)(2,1)} %get-tuple-element.48, bf16[512,4096]{1,0:T(8,128)(2,1)} %get-tuple-element.44, f32[4096]{0:T(1024)S(1)} %convert_element_type.71, f32[512]{0:T(512)S(1)} %add_rsqrt_fusion), kind=kOutput, calls=%fused_computation.5 | convolution fusion | flops 4303880192 | bytes 13649920 | tf_op jit(solution)/shard_map/cond/branch_0_fun/dot_general | solution.py:68
  63.8 4.6 convolution_convert_fusion.1
  68.4 1.4 collective-permute-start
  69.8 22.5 %collective-permute-done = bf16[512,1024]{1,0:T(8,128)(2,1)S(1)} collective-permute-done((bf16[512,1024]{1,0:T(8,128)(2,1)S(1)}, bf16[512,1024]{1,0:T(8,128)(2,1)S(1)}, u32[]{:S(2)}, u32[]{:S(2)}) %collective-permute-start) | collective-permute-done | bytes 1048608 | tf_op jit(solution)/shard_map/ppermute | solution.py:14
  92.3 1.0 copy-done.16
  93.3 0.0 all-gather.9.cloned.1.call-update
  93.3 0.0 all-gather.11.cloned.1.call-start
  93.4 4.2 collective-permute-start.1
  97.6 21.7 %collective-permute-done.1 = bf16[512,1024]{1,0:T(8,128)(2,1)S(1)} collective-permute-done((bf16[512,1024]{1,0:T(8,128)(2,1)S(1)}, bf16[512,1024]{1,0:T(8,128)(2,1)S(1)}, u32[]{:S(2)}, u32[]{:S(2)}) %collective-permute-start.1) | collective-permute-done | bytes 1048608 | tf_op jit(solution)/shard_map/ppermute | solution.py:14
  119.3 1.0 copy-done.17
  120.3 0.0 reduce-scatter.2.cloned.1.call-start
  120.4 0.0 all-gather.5.cloned.1.call-done
  120.4 0.1 conditional.6
  120.4 0.1 reshape.1084
  120.5 85.2 %all-gather.9.cloned.1.call-done = bf16[2,4096,1024]{2,1,0:T(8,128)(2,1)} async-done(((bf16[2,256,1024]{2,1,0:T(8,128)(2,1)}), bf16[2,4096,1024]{2,1,0:T(8,128)(2,1)}) %all-gather.9.cloned.1.call-update) | async-done | bytes 16777232 | tf_op jit(solution)/shard_map/all_gather | solution.py:96
  205.8 113.1 %all-gather.11.cloned.1.call-done = bf16[2,4096,1024]{2,1,0:T(8,128)(2,1)} async-done(((bf16[2,256,1024]{2,1,0:T(8,128)(2,1)}), bf16[2,4096,1024]{2,1,0:T(8,128)(2,1)}) %all-gather.11.cloned.1.call-update) | async-done | bytes 16777232 | tf_op jit(solution)/shard_map/all_gather | solution.py:97
  318.9 1.1 conditional.7
  318.9 1.1 broadcast_in_dim.245
  320.0 0.1 conditional.9
  320.0 0.1 broadcast.490
  320.1 1.0 copy-done.14
  321.2 141.0 %reduce-scatter.2.cloned.1.call-done = bf16[128,512]{1,0:T(8,128)(2,1)} async-done(((bf16[128,4096]{1,0:T(8,128)(2,1)}), bf16[128,512]{1,0:T(8,128)(2,1)}) %reduce-scatter.2.cloned.1.call-update) | async-done | bytes 131088 | tf_op jit(solution)/shard_map/reduce_scatter | solution.py:135
  462.1 1.7 add_convert_fusion
  (22 shorter events, 0.1 us)
Async XLA Ops:
  6.5 44.7 %all-gather.7.cloned.1.call-start = ((), (), s32[]{:S(2)}) async-start(), calls=%async_computation.2 | async-start | bytes 5242880 | tf_op jit(solution)/shard_map/all_gather | solution.py:54
  7.3 113.2 %all-gather.5.cloned.1.call-start = ((), (), s32[]{:S(2)}) async-start(), calls=%async_computation.1 | async-start | bytes 1310720 | tf_op jit(solution)/shard_map/all_gather | solution.py:55
  8.0 11.8 %copy-start.18 = (bf16[1,4096]{1,0:T(2,128)(2,1)S(1)}, bf16[1,4096]{1,0:T(2,128)(2,1)}, u32[]{:S(2)}) copy-start(bf16[1,4096]{1,0:T(2,128)(2,1)} %param.17) | copy-start | bytes 24580
  8.0 197.8 %all-gather.9.cloned.1.call-start = ((), (), s32[]{:S(2)}) async-start(), calls=%async_computation.3 | async-start | bytes 17825792 | tf_op jit(solution)/shard_map/all_gather | solution.py:96
  51.2 12.6 %slice-start = ((s8[8388608]{0:T(1024)(128)(4,1)}), s8[4194304]{0:T(1024)(128)(4,1)S(1)}, s32[]{:S(2)}) async-start(s8[8388608]{0:T(1024)(128)(4,1)} %bitcast.82), calls=%async_computation.6 | async-start | bytes 8388608 | tf_op jit(solution)/shard_map/cond
  54.4 9.4 %slice-start.1 = ((s8[8388608]{0:T(1024)(128)(4,1)}), s8[4194304]{0:T(1024)(128)(4,1)S(1)}, s32[]{:S(2)}) async-start(s8[8388608]{0:T(1024)(128)(4,1)} %bitcast.82), calls=%async_computation.7 | async-start | bytes 8388608 | tf_op jit(solution)/shard_map/cond
  54.4 9.4 %copy-start = (bf16[512,4096]{1,0:T(8,128)(2,1)S(1)}, bf16[512,4096]{1,0:T(8,128)(2,1)}, u32[]{:S(2)}) copy-start(bf16[512,4096]{1,0:T(8,128)(2,1)} %get-tuple-element.44) | copy-start | bytes 12582916 | tf_op jit(solution)/shard_map/cond
  68.4 23.9 %collective-permute-start = (bf16[512,1024]{1,0:T(8,128)(2,1)S(1)}, bf16[512,1024]{1,0:T(8,128)(2,1)S(1)}, u32[]{:S(2)}, u32[]{:S(2)}) collective-permute-start(bf16[512,1024]{1,0:T(8,128)(2,1)S(1)} %get-tuple-element.62), channel_id=1, source_target_pairs={{0,64},{1,65},{2,66},{3,67},{4,68},{5,69},{6,70},{7,71},{8,72},{9,... | collective-permute-start | bytes 3145736 | tf_op jit(solution)/shard_map/ppermute | solution.py:14
  92.3 1.0 copy-start.16
  93.3 225.5 %all-gather.11.cloned.1.call-start = ((), (), s32[]{:S(2)}) async-start(), calls=%async_computation.4 | async-start | bytes 17825792 | tf_op jit(solution)/shard_map/all_gather | solution.py:97
  93.4 25.9 %collective-permute-start.1 = (bf16[512,1024]{1,0:T(8,128)(2,1)S(1)}, bf16[512,1024]{1,0:T(8,128)(2,1)S(1)}, u32[]{:S(2)}, u32[]{:S(2)}) collective-permute-start(bf16[512,1024]{1,0:T(8,128)(2,1)S(1)} %get-tuple-element.63), channel_id=1, source_target_pairs={{0,64},{1,65},{2,66},{3,67},{4,68},{5,69},{6,70},{7,71},{8,72},{9,... | collective-permute-start | bytes 3145736 | tf_op jit(solution)/shard_map/ppermute | solution.py:14
  119.3 1.0 copy-start.17
  120.3 341.8 %reduce-scatter.2.cloned.1.call-start = ((), (), s32[]{:S(2)}) async-start(), calls=%async_computation.5 | async-start | bytes 1179648 | tf_op jit(solution)/shard_map/reduce_scatter | solution.py:135
  120.4 198.4 %copy-start.19 = (s32[2]{0:T(128)S(1)}, s32[2]{0:T(128)}, u32[]{:S(2)}) copy-start(s32[2]{0:T(128)} %param.19) | copy-start | bytes 28
  320.1 1.0 copy-start.14
Sparse Core Ops, SparseCore 0:
  9.0 42.1 all-gather.6
  52.9 20.7 all-gather.4
  93.5 112.2 all-gather.8
  207.8 111.0 all-gather.10
  321.3 140.8 reduce-scatter.1
where the time goes:
time: 472 us; the launch traced here: 470 us
  waiting for transfers between devices  416 us (88%)
  local copies, waits for them, and re-layouts  16 us (3%)
  matrix products  13.9 us (3%)
  between operations  13.2 us (3%)
  starting transfers between devices  5.72 us (1%)
  other arithmetic  4.95 us (1%)
    reduce_scatter x1, waiting for transfers between devices, on_device(): lax.psum_scatter(update_terms.astype(jnp.bfloat16), ('segment', 'mp'), sc...  141 us
    all_gather x1, waiting for transfers between devices, on_device(): value_part = lax.all_gather(value_flat, 'seq', axis=1, tiled=True)  113 us
    all_gather x1, waiting for transfers between devices, on_device(): key_part = lax.all_gather(key_flat, 'seq', axis=1, tiled=True)  85.2 us
    ppermute x2, waiting for transfers between devices, passed_along(): return lax.ppermute(shard, axis, pairs)  44.2 us
    all_gather x1, waiting for transfers between devices, on_device(): lax.all_gather(memory.reshape(mem_count, part_width), 'mp', axis=1, tiled...  31.4 us
    squeeze x1, local copies, waits for them, and re-layouts, on_device(): second_weight = weights[0, 1]  11.7 us
  transfers between devices with their start and end apart: 7, of which 6 were waited for; matrix products, arithmetic and copies ran while one was open for 6% of the time, Pallas kernels for 0%

commit v1 on v0

--- a/solution.py
+++ b/solution.py
@@ -93,8 +93,11 @@
         jnp.zeros((doc_count, heads_here, pos_dev, DKV), jnp.float32),
     )
     first_pos = jnp.int32(0)
-    key_part = lax.all_gather(key_flat, "seq", axis=1, tiled=True)
-    value_part = lax.all_gather(value_flat, "seq", axis=1, tiled=True)
+    key_part, value_part = jnp.split(
+        lax.all_gather(jnp.concatenate([key_flat, value_flat], axis=0), "seq", axis=1, tiled=True),
+        [key_flat.shape[0]],
+        axis=0,
+    )
     span = key_part.shape[1]
     width = 256
 

time: 472 us -> 490 us (1.038)
  local copies, waits for them, and re-layouts: 16 us -> 37 us
    split x0 -> x1, local copies, waits for them, and re-layouts: none -> 23 us  [on_device(): jnp.split(lax.all_gather(jnp.concatenate([key_flat, value_flat], axis=0),...]
    all_gather x2 -> x1, waiting for transfers between devices: 198 us -> 198 us  [on_device(): lax.all_gather(jnp.concatenate([key_flat, value_flat], axis=0), 'seq', ax...]
  transfers between devices with their start and end apart: 7 -> 6, of which waited for: 6 -> 5; matrix products, arithmetic and copies ran while one was open for 6% -> 6% of each run, Pallas kernels for 0% -> 0%
where the time goes in v1:
time: 490 us; the launch traced here: 489 us
  waiting for transfers between devices  415 us (85%)
  local copies, waits for them, and re-layouts  37 us (8%)
  matrix products  13.9 us (3%)
  between operations  13.2 us (3%)
  other arithmetic  6.48 us (1%)
    all_gather x1, waiting for transfers between devices, on_device(): lax.all_gather(jnp.concatenate([key_flat, value_flat], axis=0), 'seq', ax...  198 us
    reduce_scatter x1, waiting for transfers between devices, on_device(): lax.psum_scatter(update_terms.astype(jnp.bfloat16), ('segment', 'mp'), sc...  141 us
    ppermute x2, waiting for transfers between devices, passed_along(): return lax.ppermute(shard, axis, pairs)  43.6 us
    all_gather x1, waiting for transfers between devices, on_device(): lax.all_gather(memory.reshape(mem_count, part_width), 'mp', axis=1, tiled...  31.5 us
    split x1, local copies, waits for them, and re-layouts, on_device(): jnp.split(lax.all_gather(jnp.concatenate([key_flat, value_flat], axis=0),...  23 us
    squeeze x1, local copies, waits for them, and re-layouts, on_device(): second_weight = weights[0, 1]  11.6 us
  transfers between devices with their start and end apart: 6, of which 5 were waited for; matrix products, arithmetic and copies ran while one was open for 6% of the time, Pallas kernels for 0%

profile of v1, /device:TPU:1, one launch (start us, length us, event | category | flops | bytes accessed | tf_op | source)
XLA Modules:
  0.0 488.7 jit_solution(16031276145157775303)
XLA Ops:
  6.5 0.7 all-gather.6.cloned.1.call-update
  7.3 0.0 all-gather.4.cloned.1.call-start
  7.3 0.7 all-gather.4.cloned.1.call-update
  8.0 0.0 all-gather.8.cloned.1.call-start
  8.1 11.6 %slice_bitcast_fusion = (bf16[4096,1024]{1,0:T(8,128)(2,1)}, bf16[4096,1024]{1,0:T(8,128)(2,1)}) fusion(bf16[1,2,4096,1024]{3,2,1,0:T(8,128)(2,1)} %param.18), kind=kLoop, calls=%fused_computation.292 | loop fusion | bytes 33554432 | tf_op jit(solution)/shard_map/squeeze | solution.py:58
  19.7 0.1 reduce
  19.7 31.5 %all-gather.6.cloned.1.call-done = bf16[512,4096]{1,0:T(8,128)(2,1)} async-done(((bf16[512,1024]{1,0:T(8,128)(2,1)}), bf16[512,4096]{1,0:T(8,128)(2,1)}) %all-gather.6.cloned.1.call-update) | async-done | bytes 4194320 | tf_op jit(solution)/shard_map/all_gather | solution.py:54
  51.2 17.2 %conditional.5 = (bf16[512,1024]{1,0:T(8,128)(2,1)S(1)}, bf16[512,1024]{1,0:T(8,128)(2,1)S(1)}) conditional(s32[]{:T(128)} %convert_element_type.104, (bf16[512,4096]{1,0:T(8,128)(2,1)}, bf16[4096]{0:T(1024)(128)(2,1)S(1)}, bf16[4096,1024]{1,0:T(8,128)(2,1)}, bf16[4096,1024]{1,0:T(8,128)(2,1)}) %tuple.43, () %tuple.44), branch_computations={%region_0.0_spmd, %region_2.0_spmd} | conditional | flops 8614055936 | bytes 73468000 | solution.py:77
  51.2 3.2 fusion
  54.5 9.3 %convolution_convert_fusion = bf16[512,1024]{1,0:T(8,128)(2,1)S(1)} fusion(bf16[4096,1024]{1,0:T(8,128)(2,1)} %get-tuple-element.48, bf16[512,4096]{1,0:T(8,128)(2,1)} %get-tuple-element.44, f32[4096]{0:T(1024)S(1)} %convert_element_type.71, f32[512]{0:T(512)S(1)} %add_rsqrt_fusion), kind=kOutput, calls=%fused_computation.5 | convolution fusion | flops 4303880192 | bytes 13649920 | tf_op jit(solution)/shard_map/cond/branch_0_fun/dot_general | solution.py:68
  63.8 4.6 convolution_convert_fusion.1
  68.4 1.4 collective-permute-start
  69.8 1.4 collective-permute-start.1
  71.2 21.2 %collective-permute-done = bf16[512,1024]{1,0:T(8,128)(2,1)S(1)} collective-permute-done((bf16[512,1024]{1,0:T(8,128)(2,1)S(1)}, bf16[512,1024]{1,0:T(8,128)(2,1)S(1)}, u32[]{:S(2)}, u32[]{:S(2)}) %collective-permute-start) | collective-permute-done | bytes 1048608 | tf_op jit(solution)/shard_map/ppermute | solution.py:14
  92.3 22.5 %collective-permute-done.1 = bf16[512,1024]{1,0:T(8,128)(2,1)S(1)} collective-permute-done((bf16[512,1024]{1,0:T(8,128)(2,1)S(1)}, bf16[512,1024]{1,0:T(8,128)(2,1)S(1)}, u32[]{:S(2)}, u32[]{:S(2)}) %collective-permute-start.1) | collective-permute-done | bytes 1048608 | tf_op jit(solution)/shard_map/ppermute | solution.py:14
  114.8 1.5 pad_maximum_fusion
  116.3 0.0 all-gather.8.cloned.1.call-update
  116.4 0.0 reduce-scatter.2.cloned.1.call-start
  116.4 0.0 all-gather.4.cloned.1.call-done
  116.4 0.1 conditional.6
  116.5 0.1 reshape.1084
  116.5 0.0 copy-start.17
  116.6 198.0 %all-gather.8.cloned.1.call-done = bf16[4,4096,1024]{2,1,0:T(8,128)(2,1)} async-done(((bf16[4,256,1024]{2,1,0:T(8,128)(2,1)}), bf16[4,4096,1024]{2,1,0:T(8,128)(2,1)}) %all-gather.8.cloned.1.call-update) | async-done | bytes 33554448 | tf_op jit(solution)/shard_map/all_gather | solution.py:97
  314.6 23.0 %fusion.208 = (bf16[2,4096,1024]{2,1,0:T(8,128)(2,1)}, bf16[2,4096,1024]{2,1,0:T(8,128)(2,1)}) fusion(bf16[4,4096,1024]{2,1,0:T(8,128)(2,1)} %all-gather.8.cloned.1.call-done), kind=kLoop, calls=%fused_computation.299 | loop fusion | bytes 67108864 | tf_op jit(solution)/shard_map/split | solution.py:96
  337.6 1.1 conditional.7
  337.6 1.1 broadcast_in_dim.245
  338.8 0.1 conditional.9
  338.8 0.1 broadcast.490
  338.9 1.0 copy-done.14
  339.9 0.0 reduce-scatter.2.cloned.1.call-update
  339.9 140.6 %reduce-scatter.2.cloned.1.call-done = bf16[128,512]{1,0:T(8,128)(2,1)} async-done(((bf16[128,4096]{1,0:T(8,128)(2,1)}), bf16[128,512]{1,0:T(8,128)(2,1)}) %reduce-scatter.2.cloned.1.call-update) | async-done | bytes 131088 | tf_op jit(solution)/shard_map/reduce_scatter | solution.py:138
  480.5 1.7 add_convert_fusion
  (17 shorter events, 0.1 us)
Async XLA Ops:
  6.5 44.7 %all-gather.6.cloned.1.call-start = ((), (), s32[]{:S(2)}) async-start(), calls=%async_computation.2 | async-start | bytes 5242880 | tf_op jit(solution)/shard_map/all_gather | solution.py:54
  7.3 109.2 %all-gather.4.cloned.1.call-start = ((), (), s32[]{:S(2)}) async-start(), calls=%async_computation.1 | async-start | bytes 1310720 | tf_op jit(solution)/shard_map/all_gather | solution.py:55
  8.0 11.7 %copy-start.16 = (bf16[1,4096]{1,0:T(2,128)(2,1)S(1)}, bf16[1,4096]{1,0:T(2,128)(2,1)}, u32[]{:S(2)}) copy-start(bf16[1,4096]{1,0:T(2,128)(2,1)} %param.17) | copy-start | bytes 24580
  8.0 306.6 %all-gather.8.cloned.1.call-start = ((), (), s32[]{:S(2)}) async-start(), calls=%async_computation.3 | async-start | bytes 35651584 | tf_op jit(solution)/shard_map/all_gather | solution.py:97
  51.2 12.6 %slice-start = ((s8[8388608]{0:T(1024)(128)(4,1)}), s8[4194304]{0:T(1024)(128)(4,1)S(1)}, s32[]{:S(2)}) async-start(s8[8388608]{0:T(1024)(128)(4,1)} %bitcast.82), calls=%async_computation.5 | async-start | bytes 8388608 | tf_op jit(solution)/shard_map/cond
  54.4 9.4 %slice-start.1 = ((s8[8388608]{0:T(1024)(128)(4,1)}), s8[4194304]{0:T(1024)(128)(4,1)S(1)}, s32[]{:S(2)}) async-start(s8[8388608]{0:T(1024)(128)(4,1)} %bitcast.82), calls=%async_computation.6 | async-start | bytes 8388608 | tf_op jit(solution)/shard_map/cond
  54.4 9.4 %copy-start = (bf16[512,4096]{1,0:T(8,128)(2,1)S(1)}, bf16[512,4096]{1,0:T(8,128)(2,1)}, u32[]{:S(2)}) copy-start(bf16[512,4096]{1,0:T(8,128)(2,1)} %get-tuple-element.44) | copy-start | bytes 12582916 | tf_op jit(solution)/shard_map/cond
  68.4 23.9 %collective-permute-start = (bf16[512,1024]{1,0:T(8,128)(2,1)S(1)}, bf16[512,1024]{1,0:T(8,128)(2,1)S(1)}, u32[]{:S(2)}, u32[]{:S(2)}) collective-permute-start(bf16[512,1024]{1,0:T(8,128)(2,1)S(1)} %get-tuple-element.62), channel_id=1, source_target_pairs={{0,64},{1,65},{2,66},{3,67},{4,68},{5,69},{6,70},{7,71},{8,72},{9,... | collective-permute-start | bytes 3145736 | tf_op jit(solution)/shard_map/ppermute | solution.py:14
  69.8 45.0 %collective-permute-start.1 = (bf16[512,1024]{1,0:T(8,128)(2,1)S(1)}, bf16[512,1024]{1,0:T(8,128)(2,1)S(1)}, u32[]{:S(2)}, u32[]{:S(2)}) collective-permute-start(bf16[512,1024]{1,0:T(8,128)(2,1)S(1)} %get-tuple-element.63), channel_id=1, source_target_pairs={{0,64},{1,65},{2,66},{3,67},{4,68},{5,69},{6,70},{7,71},{8,72},{9,... | collective-permute-start | bytes 3145736 | tf_op jit(solution)/shard_map/ppermute | solution.py:14
  116.4 364.2 %reduce-scatter.2.cloned.1.call-start = ((), (), s32[]{:S(2)}) async-start(), calls=%async_computation.4 | async-start | bytes 1179648 | tf_op jit(solution)/shard_map/reduce_scatter | solution.py:138
  116.5 221.1 %copy-start.17 = (s32[2]{0:T(128)S(1)}, s32[2]{0:T(128)}, u32[]{:S(2)}) copy-start(s32[2]{0:T(128)} %param.19) | copy-start | bytes 28
  338.9 1.0 copy-start.14
Sparse Core Ops, SparseCore 0:
  9.0 42.1 all-gather.5
  52.9 20.7 all-gather.3
  116.5 198.0 all-gather.7
  340.0 140.4 reduce-scatter.1
